TPU v7x, 32 devices: a whole 2x2x4 slice. The times are simulated.
32 devices in a mesh: row: 8 (over z, x), col: 4 (over y, core).
Axes of the slice: x: 2, y: 2, z: 4, core: 2. Of those that a mesh axis runs over, the one named last changes fastest.
Arguments:
- right_side: float32 [6, 8, 64, 128], P(None, 'row'), may hold values from -6 to 6
- inverses: float32 [6, 8, 128, 128], P(None, 'row'), may hold values from -1 to 3
- factor_blocks: bfloat16 [15, 8, 8, 128, 128], P(None, 'row', 'col'), may hold values from -0.15625 to 0.15625
- pattern: int32 [15, 8, 8], P(None, 'row', 'col'), may hold values 0 or 1
Outputs:
- forward_part: float32 [6, 8, 64, 128], P(None, 'row')
- solution: float32 [6, 8, 64, 128], P(None, 'row')
All inputs are finite; a program needn't handle non-finite values. No bound on the sum of `pattern` on one device may be relied on, other than what follows from the above.
Results may differ from a plain program's by a relative error of at most 0.014.
Values may be sent and summed in bfloat16 or wider, within the bound.
No kernel may reach another device: no remote copies, remote signals or barrier semaphores. Data moves between devices by JAX's collectives and lax.ppermute only.
A program may use at most 64 MiB of HBM per device.

v0:
```python
import jax
import jax.numpy as jnp
from jax import lax
from jax.sharding import PartitionSpec as P


def spread(block, axis, holder):
    block = jnp.where(lax.axis_index(axis) == holder, block, jnp.zeros_like(block))
    return lax.psum(block, axis)


def pair_number(higher, lower_level):
    return higher * (higher - 1) // 2 + lower_level


def masked_block(factor_blocks, pattern, pair_index):
    return jnp.where(
        pattern[pair_index][:, :, None, None] != 0,
        factor_blocks[pair_index],
        jnp.zeros((), factor_blocks.dtype),
    )


def shards(right_side, inverses, factor_blocks, pattern):
    levels = right_side.shape[0]
    width_col = factor_blocks.shape[2]
    row_index = lax.axis_index("row")
    col_index = lax.axis_index("col")
    solved = []
    gathered = []
    for height in range(levels):
        remaining = right_side[height]
        if height > 0:
            partial_value = jnp.zeros(remaining.shape, jnp.float32)
            for earlier in range(height):
                masked = masked_block(factor_blocks, pattern, pair_number(height, earlier))
                partial_value = partial_value + jnp.einsum(
                    "ikab,knb->ina", masked, gathered[earlier], preferred_element_type=jnp.float32
                )
            summed = lax.psum(partial_value.astype(jnp.bfloat16), "col").astype(jnp.float32)
            remaining = remaining - summed
        segment = jnp.einsum(
            "inb,iab->ina", remaining, inverses[height], precision=lax.Precision.HIGHEST
        )
        solved.append(segment)
        if height < levels - 1:
            gathered_all = lax.all_gather(segment.astype(jnp.bfloat16), "row", axis=0, tiled=True)
            gathered.append(
                lax.dynamic_slice_in_dim(gathered_all, col_index * width_col, width_col, 0)
            )
    results = [None] * levels
    settled = [None] * levels
    for height in range(levels - 1, -1, -1):
        remaining = solved[height]
        if height < levels - 1:
            partial_value = jnp.zeros((width_col,) + remaining.shape[1:], jnp.float32)
            for later in range(height + 1, levels):
                masked = masked_block(factor_blocks, pattern, pair_number(later, height))
                partial_value = partial_value + jnp.einsum(
                    "ikab,ina->knb", masked, settled[later], preferred_element_type=jnp.float32
                )
            offset = jnp.clip(row_index - col_index * width_col, 0, width_col - 1)
            owner_col = row_index // width_col
            summed = lax.psum(partial_value, "row")
            own_sum = lax.dynamic_slice_in_dim(summed, offset, 1, 0)
            own_sum = spread(own_sum.astype(jnp.bfloat16), "col", owner_col).astype(own_sum.dtype)
            remaining = remaining - own_sum
        segment = jnp.einsum(
            "ina,iab->inb", remaining, inverses[height], precision=lax.Precision.HIGHEST
        )
        results[height] = segment
        settled[height] = segment.astype(jnp.bfloat16)
    return (jnp.stack(solved), jnp.stack(results))


def solution(mesh):
    placed = (
        P(None, "row", None, None),
        P(None, "row", None, None),
        P(None, "row", "col", None, None),
        P(None, "row", "col"),
    )
    return jax.shard_map(
        shards,
        mesh=mesh,
        in_specs=placed,
        out_specs=(P(None, "row", None, None), P(None, "row", None, None)),
        check_vma=False,
    )
```

profile of v0, /device:TPU:0, one launch (start us, length us, event | category | flops | bytes accessed | tf_op | source)
XLA Modules:
  0.0 446.8 jit_solution(956539431709333284)
XLA Ops:
  0.7 1.7 compare_reduce_fusion
  2.3 1.1 bitcast_dynamic-update-slice_fusion.10
  3.5 32.3 %all-gather = bf16[512,128]{1,0:T(8,128)(2,1)S(1)} all-gather(bf16[64,128]{1,0:T(8,128)(2,1)S(1)} %convert_element_type.125), channel_id=2, replica_groups=mesh['row'=8,'col'=4] {'row'}, dimensions={0}, use_global_device_ids=true | all-gather | bytes 147456 | tf_op jit(solution)/shard_map/all_gather | solution.py:47
  36.8 10.1 %psum.105 = bf16[1,64,128]{2,1,0:T(8,128)(2,1)S(1)} all-reduce(bf16[1,64,128]{2,1,0:T(8,128)(2,1)S(1)} %fusion.24), channel_id=1, replica_groups=mesh['row'=8,'col'=4] {'col'}, use_global_device_ids=true, to_apply=%region_0.1 | all-reduce | flops 8192 | bytes 32768 | tf_op jit(solution)/shard_map/psum | solution.py:40
  47.0 1.1 bitcast_dynamic-update-slice_fusion.9
  48.1 1.0 convolution_bitcast_fusion.15
  49.8 30.7 %all-gather.1 = bf16[512,128]{1,0:T(8,128)(2,1)S(1)} all-gather(bf16[64,128]{1,0:T(8,128)(2,1)S(1)} %convert_element_type.130), channel_id=3, replica_groups=mesh['row'=8,'col'=4] {'row'}, dimensions={0}, use_global_device_ids=true | all-gather | bytes 147456 | tf_op jit(solution)/shard_map/all_gather | solution.py:47
  80.7 10.1 %psum.106 = bf16[1,64,128]{2,1,0:T(8,128)(2,1)S(1)} all-reduce(bf16[1,64,128]{2,1,0:T(8,128)(2,1)S(1)} %fusion.23), channel_id=1, replica_groups=mesh['row'=8,'col'=4] {'col'}, use_global_device_ids=true, to_apply=%region_1.2 | all-reduce | flops 8192 | bytes 32768 | tf_op jit(solution)/shard_map/psum | solution.py:40
  92.2 30.5 %all-gather.2 = bf16[512,128]{1,0:T(8,128)(2,1)S(1)} all-gather(bf16[64,128]{1,0:T(8,128)(2,1)S(1)} %convert_element_type.135), channel_id=4, replica_groups=mesh['row'=8,'col'=4] {'row'}, dimensions={0}, use_global_device_ids=true | all-gather | bytes 147456 | tf_op jit(solution)/shard_map/all_gather | solution.py:47
  123.0 10.1 %psum.107 = bf16[1,64,128]{2,1,0:T(8,128)(2,1)S(1)} all-reduce(bf16[1,64,128]{2,1,0:T(8,128)(2,1)S(1)} %fusion.22), channel_id=1, replica_groups=mesh['row'=8,'col'=4] {'col'}, use_global_device_ids=true, to_apply=%region_2.3 | all-reduce | flops 8192 | bytes 32768 | tf_op jit(solution)/shard_map/psum | solution.py:40
  133.8 30.5 %all-gather.3 = bf16[512,128]{1,0:T(8,128)(2,1)S(1)} all-gather(bf16[64,128]{1,0:T(8,128)(2,1)S(1)} %convert_element_type.140), channel_id=5, replica_groups=mesh['row'=8,'col'=4] {'row'}, dimensions={0}, use_global_device_ids=true | all-gather | bytes 147456 | tf_op jit(solution)/shard_map/all_gather | solution.py:47
  164.8 10.1 %psum.108 = bf16[1,64,128]{2,1,0:T(8,128)(2,1)S(1)} all-reduce(bf16[1,64,128]{2,1,0:T(8,128)(2,1)S(1)} %fusion.21), channel_id=1, replica_groups=mesh['row'=8,'col'=4] {'col'}, use_global_device_ids=true, to_apply=%region_3.4 | all-reduce | flops 8192 | bytes 32768 | tf_op jit(solution)/shard_map/psum | solution.py:40
  175.2 30.5 %all-gather.4 = bf16[512,128]{1,0:T(8,128)(2,1)S(1)} all-gather(bf16[64,128]{1,0:T(8,128)(2,1)S(1)} %convert_element_type.145), channel_id=6, replica_groups=mesh['row'=8,'col'=4] {'row'}, dimensions={0}, use_global_device_ids=true | all-gather | bytes 147456 | tf_op jit(solution)/shard_map/all_gather | solution.py:47
  205.9 10.1 %psum.109 = bf16[1,64,128]{2,1,0:T(8,128)(2,1)S(1)} all-reduce(bf16[1,64,128]{2,1,0:T(8,128)(2,1)S(1)} %fusion.20), channel_id=1, replica_groups=mesh['row'=8,'col'=4] {'col'}, use_global_device_ids=true, to_apply=%region_4.5 | all-reduce | flops 8192 | bytes 32768 | tf_op jit(solution)/shard_map/psum | solution.py:40
  216.7 37.5 %psum.110 = bf16[2,64,128]{2,1,0:T(8,128)(2,1)S(1)} all-reduce(f32[2,64,128]{2,1,0:T(8,128)S(1)} %convolution_bitcast_fusion), channel_id=1, replica_groups=mesh['row'=8,'col'=4] {'row'}, use_global_device_ids=true, to_apply=%region_5.6 | all-reduce | flops 16384 | bytes 98304 | tf_op jit(solution)/shard_map/psum | solution.py:64
  254.2 10.1 %psum.111 = bf16[1,64,128]{2,1,0:T(8,128)(2,1)S(1)} all-reduce(bf16[1,64,128]{2,1,0:T(8,128)(2,1)S(1)} %fusion.221), channel_id=1, replica_groups=mesh['row'=8,'col'=4] {'col'}, use_global_device_ids=true, to_apply=%region_6.7 | all-reduce | flops 8192 | bytes 32768 | tf_op jit(solution)/shard_map/psum | solution.py:9
  264.9 33.4 %psum.112 = bf16[2,64,128]{2,1,0:T(8,128)(2,1)S(1)} all-reduce(f32[2,64,128]{2,1,0:T(8,128)S(1)} %fusion.3), channel_id=1, replica_groups=mesh['row'=8,'col'=4] {'row'}, use_global_device_ids=true, to_apply=%region_7.8 | all-reduce | flops 16384 | bytes 98304 | tf_op jit(solution)/shard_map/psum | solution.py:64
  298.3 10.1 %psum.113 = bf16[1,64,128]{2,1,0:T(8,128)(2,1)S(1)} all-reduce(bf16[1,64,128]{2,1,0:T(8,128)(2,1)S(1)} %fusion.222), channel_id=1, replica_groups=mesh['row'=8,'col'=4] {'col'}, use_global_device_ids=true, to_apply=%region_8.9 | all-reduce | flops 8192 | bytes 32768 | tf_op jit(solution)/shard_map/psum | solution.py:9
  309.2 35.3 %psum.114 = bf16[2,64,128]{2,1,0:T(8,128)(2,1)S(1)} all-reduce(f32[2,64,128]{2,1,0:T(8,128)S(1)} %fusion.2), channel_id=1, replica_groups=mesh['row'=8,'col'=4] {'row'}, use_global_device_ids=true, to_apply=%region_9.10 | all-reduce | flops 16384 | bytes 98304 | tf_op jit(solution)/shard_map/psum | solution.py:64
  344.6 10.1 %psum.115 = bf16[1,64,128]{2,1,0:T(8,128)(2,1)S(1)} all-reduce(bf16[1,64,128]{2,1,0:T(8,128)(2,1)S(1)} %fusion.223), channel_id=1, replica_groups=mesh['row'=8,'col'=4] {'col'}, use_global_device_ids=true, to_apply=%region_10.11 | all-reduce | flops 8192 | bytes 32768 | tf_op jit(solution)/shard_map/psum | solution.py:9
  355.7 33.4 %psum.116 = bf16[2,64,128]{2,1,0:T(8,128)(2,1)S(1)} all-reduce(f32[2,64,128]{2,1,0:T(8,128)S(1)} %fusion.1), channel_id=1, replica_groups=mesh['row'=8,'col'=4] {'row'}, use_global_device_ids=true, to_apply=%region_11.12 | all-reduce | flops 16384 | bytes 98304 | tf_op jit(solution)/shard_map/psum | solution.py:64
  389.1 10.1 %psum.117 = bf16[1,64,128]{2,1,0:T(8,128)(2,1)S(1)} all-reduce(bf16[1,64,128]{2,1,0:T(8,128)(2,1)S(1)} %fusion.224), channel_id=1, replica_groups=mesh['row'=8,'col'=4] {'col'}, use_global_device_ids=true, to_apply=%region_12.13 | all-reduce | flops 8192 | bytes 32768 | tf_op jit(solution)/shard_map/psum | solution.py:9
  400.4 35.3 %psum.118 = bf16[2,64,128]{2,1,0:T(8,128)(2,1)S(1)} all-reduce(f32[2,64,128]{2,1,0:T(8,128)S(1)} %fusion), channel_id=1, replica_groups=mesh['row'=8,'col'=4] {'row'}, use_global_device_ids=true, to_apply=%region_13.14 | all-reduce | flops 16384 | bytes 98304 | tf_op jit(solution)/shard_map/psum | solution.py:64
  435.8 10.1 %psum.119 = bf16[1,64,128]{2,1,0:T(8,128)(2,1)S(1)} all-reduce(bf16[1,64,128]{2,1,0:T(8,128)(2,1)S(1)} %fusion.225), channel_id=1, replica_groups=mesh['row'=8,'col'=4] {'col'}, use_global_device_ids=true, to_apply=%region_14.15 | all-reduce | flops 8192 | bytes 32768 | tf_op jit(solution)/shard_map/psum | solution.py:9
  (64 shorter events, 10.2 us)
Async XLA Ops:
  0.6 48.5 %copy-start = (bf16[15,1,2,128,128]{4,3,2,1,0:T(8,128)(2,1)S(1)}, bf16[15,1,2,128,128]{4,3,2,1,0:T(8,128)(2,1)}, u32[]{:S(2)}) copy-start(bf16[15,1,2,128,128]{4,3,2,1,0:T(8,128)(2,1)} %param.6) | copy-start | bytes 2949124
  49.8 41.7 %copy-start.1 = (f32[6,1,128,128]{3,2,1,0:T(8,128)S(1)}, f32[6,1,128,128]{3,2,1,0:T(8,128)}, u32[]{:S(2)}) copy-start(f32[6,1,128,128]{3,2,1,0:T(8,128)} %param.5) | copy-start | bytes 1179652
  91.0 1.0 copy-start.2
  216.3 37.9 %copy-start.3 = (f32[6,1,64,128]{3,2,1,0:T(8,128)}, f32[6,1,64,128]{3,2,1,0:T(8,128)S(1)}, u32[]{:S(2)}) copy-start(f32[6,1,64,128]{3,2,1,0:T(8,128)S(1)} %get-tuple-element.27) | copy-start | bytes 589828
  446.1 0.7 copy-start.4
where the time goes:
time: 448 us; the launch traced here: 447 us
  blocking collectives  431 us (96%)
  matrix products  12.2 us (3%)
    psum x5, blocking collectives, shards(): summed = lax.psum(partial_value, 'row')  175 us
    all_gather x5, blocking collectives, shards(): lax.all_gather(segment.astype(jnp.bfloat16), 'row', axis=0, tiled=True)  155 us
    psum x5, blocking collectives, shards(): lax.psum(partial_value.astype(jnp.bfloat16), 'col').astype(jnp.float32)  50.7 us
    psum x5, blocking collectives, spread(): return lax.psum(block, axis)  50.6 us

commit v1 on v0

--- a/solution.py
+++ b/solution.py
@@ -44,7 +44,19 @@
         )
         solved.append(segment)
         if height < levels - 1:
-            gathered_all = lax.all_gather(segment.astype(jnp.bfloat16), "row", axis=0, tiled=True)
+            array = segment.astype(jnp.bfloat16)
+            ways, here, step = (lax.axis_size("row"), lax.axis_index("row"), array.shape[0])
+            line, have = (array, 1)
+            while have < ways:
+                line = jnp.concatenate(
+                    [
+                        line,
+                        lax.ppermute(line, "row", [(d, (d - have) % ways) for d in range(ways)]),
+                    ],
+                    axis=0,
+                )
+                have = 2 * have
+            gathered_all = jnp.roll(line, here * step, axis=0)
             gathered.append(
                 lax.dynamic_slice_in_dim(gathered_all, col_index * width_col, width_col, 0)
             )

time: 448 us -> 378 us (0.84)
  blocking collectives: 431 us -> 278 us
  waiting for transfers between devices: 0 us -> 47.3 us
  starting transfers between devices: 0 us -> 36.6 us
    all_gather x5 -> x0, blocking collectives: 155 us -> none  [shards(): lax.all_gather(segment.astype(jnp.bfloat16), 'row', axis=0, tiled=True)]
    ppermute x0 -> x15, waiting for transfers between devices: none -> 47.3 us  [shards(): lax.ppermute(line, 'row', [(d, (d - have) % ways) for d in range(ways)])]
    ppermute x0 -> x15, starting transfers between devices: none -> 36.6 us  [shards(): lax.ppermute(line, 'row', [(d, (d - have) % ways) for d in range(ways)])]
  transfers between devices with their start and end apart: 0 -> 15, of which waited for: 0 -> 15; matrix products, arithmetic and copies ran while one was open for 0% -> 1% of each run, Pallas kernels for 0% -> 0%
where the time goes in v1:
time: 378 us; the launch traced here: 377 us
  blocking collectives  278 us (74%)
  waiting for transfers between devices  47.3 us (13%)
  starting transfers between devices  36.6 us (10%)
  matrix products  11.3 us (3%)
    psum x5, blocking collectives, shards(): summed = lax.psum(partial_value, 'row')  177 us
    psum x5, blocking collectives, shards(): lax.psum(partial_value.astype(jnp.bfloat16), 'col').astype(jnp.float32)  50.7 us
    psum x5, blocking collectives, spread(): return lax.psum(block, axis)  50.6 us
    ppermute x15, waiting for transfers between devices, shards(): lax.ppermute(line, 'row', [(d, (d - have) % ways) for d in range(ways)])  47.3 us
    ppermute x15, starting transfers between devices, shards(): lax.ppermute(line, 'row', [(d, (d - have) % ways) for d in range(ways)])  36.6 us
  transfers between devices with their start and end apart: 15, of which 15 were waited for; matrix products, arithmetic and copies ran while one was open for 1% of the time, Pallas kernels for 0%

profile of v1, /device:TPU:0, one launch (start us, length us, event | category | flops | bytes accessed | tf_op | source)
XLA Modules:
  0.0 377.2 jit_solution(11090567173601093742)
XLA Ops:
  1.8 6.1 %collective-permute-start = (bf16[1,64,128]{2,1,0:T(8,128)(2,1)S(1)}, bf16[1,64,128]{2,1,0:T(8,128)(2,1)S(1)}, u32[]{:S(2)}, u32[]{:S(2)}) collective-permute-start(bf16[1,64,128]{2,1,0:T(8,128)(2,1)S(1)} %convert_bitcast_fusion.4), channel_id=1, source_target_pairs={{0,28},{4,0},{8,4},{12,8},{16,12},{20,16},{24,20},{28,24},{1,29},{... | collective-permute-start | bytes 49160 | tf_op jit(solution)/shard_map/ppermute | solution.py:54
  20.3 10.1 %psum.105 = bf16[1,64,128]{2,1,0:T(8,128)(2,1)S(1)} all-reduce(bf16[1,64,128]{2,1,0:T(8,128)(2,1)S(1)} %fusion.24), channel_id=1, replica_groups=mesh['row'=8,'col'=4] {'col'}, use_global_device_ids=true, to_apply=%region_0.2 | all-reduce | flops 8192 | bytes 32768 | tf_op jit(solution)/shard_map/psum | solution.py:40
  31.6 6.2 %collective-permute-start.3 = (bf16[1,64,128]{2,1,0:T(8,128)(2,1)S(1)}, bf16[1,64,128]{2,1,0:T(8,128)(2,1)S(1)}, u32[]{:S(2)}, u32[]{:S(2)}) collective-permute-start(bf16[1,64,128]{2,1,0:T(8,128)(2,1)S(1)} %convert_bitcast_fusion.3), channel_id=1, source_target_pairs={{0,28},{4,0},{8,4},{12,8},{16,12},{20,16},{24,20},{28,24},{1,29},{... | collective-permute-start | bytes 49160 | tf_op jit(solution)/shard_map/ppermute | solution.py:54
  43.5 5.6 %collective-permute-done.5 = bf16[4,64,128]{2,1,0:T(8,128)(2,1)S(1)} collective-permute-done((bf16[4,64,128]{2,1,0:T(8,128)(2,1)S(1)}, bf16[4,64,128]{2,1,0:T(8,128)(2,1)S(1)}, u32[]{:S(2)}, u32[]{:S(2)}) %collective-permute-start.5) | collective-permute-done | bytes 65568 | tf_op jit(solution)/shard_map/ppermute | solution.py:54
  49.4 10.1 %psum.106 = bf16[1,64,128]{2,1,0:T(8,128)(2,1)S(1)} all-reduce(bf16[1,64,128]{2,1,0:T(8,128)(2,1)S(1)} %fusion.23), channel_id=1, replica_groups=mesh['row'=8,'col'=4] {'col'}, use_global_device_ids=true, to_apply=%region_1.3 | all-reduce | flops 8192 | bytes 32768 | tf_op jit(solution)/shard_map/psum | solution.py:40
  59.8 6.3 %collective-permute-start.6 = (bf16[1,64,128]{2,1,0:T(8,128)(2,1)S(1)}, bf16[1,64,128]{2,1,0:T(8,128)(2,1)S(1)}, u32[]{:S(2)}, u32[]{:S(2)}) collective-permute-start(bf16[1,64,128]{2,1,0:T(8,128)(2,1)S(1)} %convert_bitcast_fusion.2), channel_id=1, source_target_pairs={{0,28},{4,0},{8,4},{12,8},{16,12},{20,16},{24,20},{28,24},{1,29},{... | collective-permute-start | bytes 49160 | tf_op jit(solution)/shard_map/ppermute | solution.py:54
  71.8 5.7 %collective-permute-done.8 = bf16[4,64,128]{2,1,0:T(8,128)(2,1)S(1)} collective-permute-done((bf16[4,64,128]{2,1,0:T(8,128)(2,1)S(1)}, bf16[4,64,128]{2,1,0:T(8,128)(2,1)S(1)}, u32[]{:S(2)}, u32[]{:S(2)}) %collective-permute-start.8) | collective-permute-done | bytes 65568 | tf_op jit(solution)/shard_map/ppermute | solution.py:54
  77.7 10.1 %psum.107 = bf16[1,64,128]{2,1,0:T(8,128)(2,1)S(1)} all-reduce(bf16[1,64,128]{2,1,0:T(8,128)(2,1)S(1)} %fusion.22), channel_id=1, replica_groups=mesh['row'=8,'col'=4] {'col'}, use_global_device_ids=true, to_apply=%region_2.4 | all-reduce | flops 8192 | bytes 32768 | tf_op jit(solution)/shard_map/psum | solution.py:40
  88.1 6.3 %collective-permute-start.9 = (bf16[1,64,128]{2,1,0:T(8,128)(2,1)S(1)}, bf16[1,64,128]{2,1,0:T(8,128)(2,1)S(1)}, u32[]{:S(2)}, u32[]{:S(2)}) collective-permute-start(bf16[1,64,128]{2,1,0:T(8,128)(2,1)S(1)} %convert_bitcast_fusion.1), channel_id=1, source_target_pairs={{0,28},{4,0},{8,4},{12,8},{16,12},{20,16},{24,20},{28,24},{1,29},{... | collective-permute-start | bytes 49160 | tf_op jit(solution)/shard_map/ppermute | solution.py:54
  100.0 5.7 %collective-permute-done.11 = bf16[4,64,128]{2,1,0:T(8,128)(2,1)S(1)} collective-permute-done((bf16[4,64,128]{2,1,0:T(8,128)(2,1)S(1)}, bf16[4,64,128]{2,1,0:T(8,128)(2,1)S(1)}, u32[]{:S(2)}, u32[]{:S(2)}) %collective-permute-start.11) | collective-permute-done | bytes 65568 | tf_op jit(solution)/shard_map/ppermute | solution.py:54
  106.0 10.1 %psum.108 = bf16[1,64,128]{2,1,0:T(8,128)(2,1)S(1)} all-reduce(bf16[1,64,128]{2,1,0:T(8,128)(2,1)S(1)} %fusion.21), channel_id=1, replica_groups=mesh['row'=8,'col'=4] {'col'}, use_global_device_ids=true, to_apply=%region_3.5 | all-reduce | flops 8192 | bytes 32768 | tf_op jit(solution)/shard_map/psum | solution.py:40
  116.4 6.3 %collective-permute-start.12 = (bf16[1,64,128]{2,1,0:T(8,128)(2,1)S(1)}, bf16[1,64,128]{2,1,0:T(8,128)(2,1)S(1)}, u32[]{:S(2)}, u32[]{:S(2)}) collective-permute-start(bf16[1,64,128]{2,1,0:T(8,128)(2,1)S(1)} %convert_bitcast_fusion), channel_id=1, source_target_pairs={{0,28},{4,0},{8,4},{12,8},{16,12},{20,16},{24,20},{28,24},{1,29},{... | collective-permute-start | bytes 49160 | tf_op jit(solution)/shard_map/ppermute | solution.py:54
  128.3 5.7 %collective-permute-done.14 = bf16[4,64,128]{2,1,0:T(8,128)(2,1)S(1)} collective-permute-done((bf16[4,64,128]{2,1,0:T(8,128)(2,1)S(1)}, bf16[4,64,128]{2,1,0:T(8,128)(2,1)S(1)}, u32[]{:S(2)}, u32[]{:S(2)}) %collective-permute-start.14) | collective-permute-done | bytes 65568 | tf_op jit(solution)/shard_map/ppermute | solution.py:54
  134.2 10.1 %psum.109 = bf16[1,64,128]{2,1,0:T(8,128)(2,1)S(1)} all-reduce(bf16[1,64,128]{2,1,0:T(8,128)(2,1)S(1)} %fusion.20), channel_id=1, replica_groups=mesh['row'=8,'col'=4] {'col'}, use_global_device_ids=true, to_apply=%region_4.6 | all-reduce | flops 8192 | bytes 32768 | tf_op jit(solution)/shard_map/psum | solution.py:40
  145.0 39.6 %psum.110 = bf16[2,64,128]{2,1,0:T(8,128)(2,1)S(1)} all-reduce(f32[2,64,128]{2,1,0:T(8,128)S(1)} %convolution_bitcast_fusion), channel_id=1, replica_groups=mesh['row'=8,'col'=4] {'row'}, use_global_device_ids=true, to_apply=%region_5.7 | all-reduce | flops 16384 | bytes 98304 | tf_op jit(solution)/shard_map/psum | solution.py:76
  184.5 10.1 %psum.111 = bf16[1,64,128]{2,1,0:T(8,128)(2,1)S(1)} all-reduce(bf16[1,64,128]{2,1,0:T(8,128)(2,1)S(1)} %fusion.252), channel_id=1, replica_groups=mesh['row'=8,'col'=4] {'col'}, use_global_device_ids=true, to_apply=%region_6.8 | all-reduce | flops 8192 | bytes 32768 | tf_op jit(solution)/shard_map/psum | solution.py:9
  195.3 33.4 %psum.112 = bf16[2,64,128]{2,1,0:T(8,128)(2,1)S(1)} all-reduce(f32[2,64,128]{2,1,0:T(8,128)S(1)} %fusion.3), channel_id=1, replica_groups=mesh['row'=8,'col'=4] {'row'}, use_global_device_ids=true, to_apply=%region_7.9 | all-reduce | flops 16384 | bytes 98304 | tf_op jit(solution)/shard_map/psum | solution.py:76
  228.7 10.1 %psum.113 = bf16[1,64,128]{2,1,0:T(8,128)(2,1)S(1)} all-reduce(bf16[1,64,128]{2,1,0:T(8,128)(2,1)S(1)} %fusion.253), channel_id=1, replica_groups=mesh['row'=8,'col'=4] {'col'}, use_global_device_ids=true, to_apply=%region_8.10 | all-reduce | flops 8192 | bytes 32768 | tf_op jit(solution)/shard_map/psum | solution.py:9
  239.6 35.3 %psum.114 = bf16[2,64,128]{2,1,0:T(8,128)(2,1)S(1)} all-reduce(f32[2,64,128]{2,1,0:T(8,128)S(1)} %fusion.2), channel_id=1, replica_groups=mesh['row'=8,'col'=4] {'row'}, use_global_device_ids=true, to_apply=%region_9.11 | all-reduce | flops 16384 | bytes 98304 | tf_op jit(solution)/shard_map/psum | solution.py:76
  274.9 10.1 %psum.115 = bf16[1,64,128]{2,1,0:T(8,128)(2,1)S(1)} all-reduce(bf16[1,64,128]{2,1,0:T(8,128)(2,1)S(1)} %fusion.254), channel_id=1, replica_groups=mesh['row'=8,'col'=4] {'col'}, use_global_device_ids=true, to_apply=%region_10.12 | all-reduce | flops 8192 | bytes 32768 | tf_op jit(solution)/shard_map/psum | solution.py:9
  286.1 33.4 %psum.116 = bf16[2,64,128]{2,1,0:T(8,128)(2,1)S(1)} all-reduce(f32[2,64,128]{2,1,0:T(8,128)S(1)} %fusion.1), channel_id=1, replica_groups=mesh['row'=8,'col'=4] {'row'}, use_global_device_ids=true, to_apply=%region_11.13 | all-reduce | flops 16384 | bytes 98304 | tf_op jit(solution)/shard_map/psum | solution.py:76
  319.5 10.1 %psum.117 = bf16[1,64,128]{2,1,0:T(8,128)(2,1)S(1)} all-reduce(bf16[1,64,128]{2,1,0:T(8,128)(2,1)S(1)} %fusion.255), channel_id=1, replica_groups=mesh['row'=8,'col'=4] {'col'}, use_global_device_ids=true, to_apply=%region_12.14 | all-reduce | flops 8192 | bytes 32768 | tf_op jit(solution)/shard_map/psum | solution.py:9
  330.8 35.3 %psum.118 = bf16[2,64,128]{2,1,0:T(8,128)(2,1)S(1)} all-reduce(f32[2,64,128]{2,1,0:T(8,128)S(1)} %fusion), channel_id=1, replica_groups=mesh['row'=8,'col'=4] {'row'}, use_global_device_ids=true, to_apply=%region_13.15 | all-reduce | flops 16384 | bytes 98304 | tf_op jit(solution)/shard_map/psum | solution.py:76
  366.1 10.1 %psum.119 = bf16[1,64,128]{2,1,0:T(8,128)(2,1)S(1)} all-reduce(bf16[1,64,128]{2,1,0:T(8,128)(2,1)S(1)} %fusion.256), channel_id=1, replica_groups=mesh['row'=8,'col'=4] {'col'}, use_global_device_ids=true, to_apply=%region_14.16 | all-reduce | flops 8192 | bytes 32768 | tf_op jit(solution)/shard_map/psum | solution.py:9
  (103 shorter events, 44.2 us)
Async XLA Ops:
  0.6 42.6 %copy-start = (bf16[15,1,2,128,128]{4,3,2,1,0:T(8,128)(2,1)S(1)}, bf16[15,1,2,128,128]{4,3,2,1,0:T(8,128)(2,1)}, u32[]{:S(2)}) copy-start(bf16[15,1,2,128,128]{4,3,2,1,0:T(8,128)(2,1)} %param.8) | copy-start | bytes 2949124
  1.8 7.5 %collective-permute-start = (bf16[1,64,128]{2,1,0:T(8,128)(2,1)S(1)}, bf16[1,64,128]{2,1,0:T(8,128)(2,1)S(1)}, u32[]{:S(2)}, u32[]{:S(2)}) collective-permute-start(bf16[1,64,128]{2,1,0:T(8,128)(2,1)S(1)} %convert_bitcast_fusion.4), channel_id=1, source_target_pairs={{0,28},{4,0},{8,4},{12,8},{16,12},{20,16},{24,20},{28,24},{1,29},{... | collective-permute-start | bytes 49160 | tf_op jit(solution)/shard_map/ppermute | solution.py:54
  9.3 3.9 %collective-permute-start.1 = (bf16[2,64,128]{2,1,0:T(8,128)(2,1)S(1)}, bf16[2,64,128]{2,1,0:T(8,128)(2,1)S(1)}, u32[]{:S(2)}, u32[]{:S(2)}) collective-permute-start(bf16[2,64,128]{2,1,0:T(8,128)(2,1)S(1)} %pad_maximum_fusion.5), channel_id=1, source_target_pairs={{0,24},{4,28},{8,0},{12,4},{16,8},{20,12},{24,16},{28,20},{1,25},{... | collective-permute-start | bytes 98312 | tf_op jit(solution)/shard_map/ppermute | solution.py:54
  13.3 5.9 %collective-permute-start.2 = (bf16[4,64,128]{2,1,0:T(8,128)(2,1)S(1)}, bf16[4,64,128]{2,1,0:T(8,128)(2,1)S(1)}, u32[]{:S(2)}, u32[]{:S(2)}) collective-permute-start(bf16[4,64,128]{2,1,0:T(8,128)(2,1)S(1)} %pad_maximum_fusion), channel_id=1, source_target_pairs={{0,16},{4,20},{8,24},{12,28},{16,0},{20,4},{24,8},{28,12},{1,17},{... | collective-permute-start | bytes 196616 | tf_op jit(solution)/shard_map/ppermute | solution.py:54
  31.6 28.0 %copy-start.1 = (f32[6,1,128,128]{3,2,1,0:T(8,128)S(1)}, f32[6,1,128,128]{3,2,1,0:T(8,128)}, u32[]{:S(2)}) copy-start(f32[6,1,128,128]{3,2,1,0:T(8,128)} %param.7) | copy-start | bytes 1179652
  31.6 7.7 %collective-permute-start.3 = (bf16[1,64,128]{2,1,0:T(8,128)(2,1)S(1)}, bf16[1,64,128]{2,1,0:T(8,128)(2,1)S(1)}, u32[]{:S(2)}, u32[]{:S(2)}) collective-permute-start(bf16[1,64,128]{2,1,0:T(8,128)(2,1)S(1)} %convert_bitcast_fusion.3), channel_id=1, source_target_pairs={{0,28},{4,0},{8,4},{12,8},{16,12},{20,16},{24,20},{28,24},{1,29},{... | collective-permute-start | bytes 49160 | tf_op jit(solution)/shard_map/ppermute | solution.py:54
  39.3 3.9 %collective-permute-start.4 = (bf16[2,64,128]{2,1,0:T(8,128)(2,1)S(1)}, bf16[2,64,128]{2,1,0:T(8,128)(2,1)S(1)}, u32[]{:S(2)}, u32[]{:S(2)}) collective-permute-start(bf16[2,64,128]{2,1,0:T(8,128)(2,1)S(1)} %pad_maximum_fusion.6), channel_id=1, source_target_pairs={{0,24},{4,28},{8,0},{12,4},{16,8},{20,12},{24,16},{28,20},{1,25},{... | collective-permute-start | bytes 98312 | tf_op jit(solution)/shard_map/ppermute | solution.py:54
  43.2 5.9 %collective-permute-start.5 = (bf16[4,64,128]{2,1,0:T(8,128)(2,1)S(1)}, bf16[4,64,128]{2,1,0:T(8,128)(2,1)S(1)}, u32[]{:S(2)}, u32[]{:S(2)}) collective-permute-start(bf16[4,64,128]{2,1,0:T(8,128)(2,1)S(1)} %pad_maximum_fusion.1), channel_id=1, source_target_pairs={{0,16},{4,20},{8,24},{12,28},{16,0},{20,4},{24,8},{28,12},{1,17},{... | collective-permute-start | bytes 196616 | tf_op jit(solution)/shard_map/ppermute | solution.py:54
  43.5 16.1 %copy-start.2 = (f32[6,1,64,128]{3,2,1,0:T(8,128)S(1)}, f32[6,1,64,128]{3,2,1,0:T(8,128)}, u32[]{:S(2)}) copy-start(f32[6,1,64,128]{3,2,1,0:T(8,128)} %param.6) | copy-start | bytes 589828
  59.8 7.8 %collective-permute-start.6 = (bf16[1,64,128]{2,1,0:T(8,128)(2,1)S(1)}, bf16[1,64,128]{2,1,0:T(8,128)(2,1)S(1)}, u32[]{:S(2)}, u32[]{:S(2)}) collective-permute-start(bf16[1,64,128]{2,1,0:T(8,128)(2,1)S(1)} %convert_bitcast_fusion.2), channel_id=1, source_target_pairs={{0,28},{4,0},{8,4},{12,8},{16,12},{20,16},{24,20},{28,24},{1,29},{... | collective-permute-start | bytes 49160 | tf_op jit(solution)/shard_map/ppermute | solution.py:54
  67.5 3.9 %collective-permute-start.7 = (bf16[2,64,128]{2,1,0:T(8,128)(2,1)S(1)}, bf16[2,64,128]{2,1,0:T(8,128)(2,1)S(1)}, u32[]{:S(2)}, u32[]{:S(2)}) collective-permute-start(bf16[2,64,128]{2,1,0:T(8,128)(2,1)S(1)} %pad_maximum_fusion.7), channel_id=1, source_target_pairs={{0,24},{4,28},{8,0},{12,4},{16,8},{20,12},{24,16},{28,20},{1,25},{... | collective-permute-start | bytes 98312 | tf_op jit(solution)/shard_map/ppermute | solution.py:54
  71.5 5.9 %collective-permute-start.8 = (bf16[4,64,128]{2,1,0:T(8,128)(2,1)S(1)}, bf16[4,64,128]{2,1,0:T(8,128)(2,1)S(1)}, u32[]{:S(2)}, u32[]{:S(2)}) collective-permute-start(bf16[4,64,128]{2,1,0:T(8,128)(2,1)S(1)} %pad_maximum_fusion.2), channel_id=1, source_target_pairs={{0,16},{4,20},{8,24},{12,28},{16,0},{20,4},{24,8},{28,12},{1,17},{... | collective-permute-start | bytes 196616 | tf_op jit(solution)/shard_map/ppermute | solution.py:54
  88.1 7.8 %collective-permute-start.9 = (bf16[1,64,128]{2,1,0:T(8,128)(2,1)S(1)}, bf16[1,64,128]{2,1,0:T(8,128)(2,1)S(1)}, u32[]{:S(2)}, u32[]{:S(2)}) collective-permute-start(bf16[1,64,128]{2,1,0:T(8,128)(2,1)S(1)} %convert_bitcast_fusion.1), channel_id=1, source_target_pairs={{0,28},{4,0},{8,4},{12,8},{16,12},{20,16},{24,20},{28,24},{1,29},{... | collective-permute-start | bytes 49160 | tf_op jit(solution)/shard_map/ppermute | solution.py:54
  95.8 3.9 %collective-permute-start.10 = (bf16[2,64,128]{2,1,0:T(8,128)(2,1)S(1)}, bf16[2,64,128]{2,1,0:T(8,128)(2,1)S(1)}, u32[]{:S(2)}, u32[]{:S(2)}) collective-permute-start(bf16[2,64,128]{2,1,0:T(8,128)(2,1)S(1)} %pad_maximum_fusion.8), channel_id=1, source_target_pairs={{0,24},{4,28},{8,0},{12,4},{16,8},{20,12},{24,16},{28,20},{1,25},{... | collective-permute-start | bytes 98312 | tf_op jit(solution)/shard_map/ppermute | solution.py:54
  99.8 5.9 %collective-permute-start.11 = (bf16[4,64,128]{2,1,0:T(8,128)(2,1)S(1)}, bf16[4,64,128]{2,1,0:T(8,128)(2,1)S(1)}, u32[]{:S(2)}, u32[]{:S(2)}) collective-permute-start(bf16[4,64,128]{2,1,0:T(8,128)(2,1)S(1)} %pad_maximum_fusion.3), channel_id=1, source_target_pairs={{0,16},{4,20},{8,24},{12,28},{16,0},{20,4},{24,8},{28,12},{1,17},{... | collective-permute-start | bytes 196616 | tf_op jit(solution)/shard_map/ppermute | solution.py:54
  116.4 7.8 %collective-permute-start.12 = (bf16[1,64,128]{2,1,0:T(8,128)(2,1)S(1)}, bf16[1,64,128]{2,1,0:T(8,128)(2,1)S(1)}, u32[]{:S(2)}, u32[]{:S(2)}) collective-permute-start(bf16[1,64,128]{2,1,0:T(8,128)(2,1)S(1)} %convert_bitcast_fusion), channel_id=1, source_target_pairs={{0,28},{4,0},{8,4},{12,8},{16,12},{20,16},{24,20},{28,24},{1,29},{... | collective-permute-start | bytes 49160 | tf_op jit(solution)/shard_map/ppermute | solution.py:54
  124.1 3.9 %collective-permute-start.13 = (bf16[2,64,128]{2,1,0:T(8,128)(2,1)S(1)}, bf16[2,64,128]{2,1,0:T(8,128)(2,1)S(1)}, u32[]{:S(2)}, u32[]{:S(2)}) collective-permute-start(bf16[2,64,128]{2,1,0:T(8,128)(2,1)S(1)} %pad_maximum_fusion.9), channel_id=1, source_target_pairs={{0,24},{4,28},{8,0},{12,4},{16,8},{20,12},{24,16},{28,20},{1,25},{... | collective-permute-start | bytes 98312 | tf_op jit(solution)/shard_map/ppermute | solution.py:54
  128.0 5.9 %collective-permute-start.14 = (bf16[4,64,128]{2,1,0:T(8,128)(2,1)S(1)}, bf16[4,64,128]{2,1,0:T(8,128)(2,1)S(1)}, u32[]{:S(2)}, u32[]{:S(2)}) collective-permute-start(bf16[4,64,128]{2,1,0:T(8,128)(2,1)S(1)} %pad_maximum_fusion.4), channel_id=1, source_target_pairs={{0,16},{4,20},{8,24},{12,28},{16,0},{20,4},{24,8},{28,12},{1,17},{... | collective-permute-start | bytes 196616 | tf_op jit(solution)/shard_map/ppermute | solution.py:54
  144.6 40.0 %copy-start.3 = (f32[6,1,64,128]{3,2,1,0:T(8,128)}, f32[6,1,64,128]{3,2,1,0:T(8,128)S(1)}, u32[]{:S(2)}) copy-start(f32[6,1,64,128]{3,2,1,0:T(8,128)S(1)} %get-tuple-element.28) | copy-start | bytes 589828
  376.5 0.7 copy-start.4
